TPU v7x, 32 devices: a whole 2x2x4 slice. The times are simulated.
32 devices in a mesh: batch: 4 (over z), seq: 8 (over y, x, core).
Axes of the slice: x: 2, y: 2, z: 4, core: 2. Of those that a mesh axis runs over, the one named last changes fastest.
Arguments:
- inputs: bfloat16 [4, 2048, 2048], P('batch', 'seq'), may hold values from -6 to 6
- segment_ids: int32 [4, 2048], P('batch'), may hold values from 0 to 3, never falling along the last dimension, each value on 1 to 1024 neighbouring positions
- w_qkv: bfloat16 [6144, 2048], P('seq'), may hold values from -0.125 to 0.125
- w_out: bfloat16 [2048, 2048], P('seq'), may hold values from -0.125 to 0.125
- w_up: bfloat16 [8192, 2048], P('seq'), may hold values from -0.125 to 0.125
- w_down: bfloat16 [2048, 8192], P('seq'), may hold values from -0.0625 to 0.0625
- gain_attn: float32 [2048], replicated, may hold values from 0.5 to 1.5
- gain_mix: float32 [2048], replicated, may hold values from 0.5 to 1.5
- gain_ffn: float32 [2048], replicated, may hold values from 0.5 to 1.5
- gain_hidden: float32 [8192], replicated, may hold values from 0.5 to 1.5
- cotangent: bfloat16 [4, 2048, 2048], P('batch', 'seq'), may hold values from -6 to 6
Outputs:
- outputs: bfloat16 [4, 2048, 2048], P('batch', 'seq')
- grad_inputs: float32 [4, 2048, 2048], P('batch', 'seq')
- grad_w_qkv: float32 [6144, 2048], P('seq')
- grad_w_out: float32 [2048, 2048], P('seq')
- grad_w_up: float32 [8192, 2048], P('seq')
- grad_w_down: float32 [2048, 8192], P('seq')
- grad_gain_attn: float32 [2048], replicated
- grad_gain_mix: float32 [2048], replicated
- grad_gain_ffn: float32 [2048], replicated
- grad_gain_hidden: float32 [8192], replicated
Inputs may be any that keep to these rules, and one draw needn't show every extreme that they name: `segment_ids`: along a row the ids never fall and each id from 0 to 3 marks one document of 1 to 1024 tokens.
All inputs are finite; a program needn't handle non-finite values.
Results may differ from a plain program's by a relative error of at most 0.02.
Values may be sent and summed in bfloat16 or wider, within the bound.
A program may use at most 448 MiB of HBM per device.

v0:
```python
import math
import jax
import jax.numpy as jnp
from jax import lax
from jax.sharding import PartitionSpec as P

HEADS = 32
HEAD_DIM = 64
LENGTH = 2048
QBLOCK = 512
XBASE = 512
EPSILON = 1e-05
MASKED = -1e30


def norm_rows(values, gain):
    average = jnp.mean(values, axis=-1, keepdims=True)
    centered = values - average
    spread = jnp.mean(centered * centered, axis=-1, keepdims=True)
    return centered * lax.rsqrt(spread + EPSILON) * gain


def gelu_norm(upper, gain):
    return norm_rows(jax.nn.gelu(upper, approximate=False), gain)


def doc_positions(seg_row):
    index = jnp.arange(seg_row.shape[0], dtype=jnp.int32)
    change = jnp.concatenate([jnp.ones((1,), dtype=bool), seg_row[1:] != seg_row[:-1]])
    starts = jnp.where(change, index, jnp.zeros_like(index))
    return index - lax.cummax(starts, axis=0)


def xpos_tables(positions):
    half_dim = HEAD_DIM // 2
    channel = jnp.arange(half_dim, dtype=jnp.float32)
    inverse = jnp.exp(channel * (-math.log(10000.0) / half_dim))
    zeta = (channel * (2.0 / HEAD_DIM) + 0.4) / 1.4
    place = positions.astype(jnp.float32)[..., None]
    angle = place * inverse
    growth = jnp.exp((place - 0.5 * LENGTH) * (1.0 / XBASE) * jnp.log(zeta))
    return (jnp.cos(angle), jnp.sin(angle), growth)


def rotate(values, cosine, sine, growth):
    half_dim = values.shape[-1] // 2
    first = values[..., :half_dim]
    second = values[..., half_dim:]
    cosine = cosine[..., None, :]
    sine = sine[..., None, :]
    growth = growth[..., None, :]
    return jnp.concatenate(
        [(first * cosine - second * sine) * growth, (second * cosine + first * sine) * growth],
        axis=-1,
    )


def allowed_pairs(seg_row, start, count):
    seg_block = lax.dynamic_slice_in_dim(seg_row, start, count, 0)
    query_place = start + jnp.arange(count, dtype=jnp.int32)
    key_place = jnp.arange(seg_row.shape[0], dtype=jnp.int32)
    return (seg_block[:, None] == seg_row[None, :]) & (key_place[None, :] <= query_place[:, None])


def block_scores(query_block, keys, allowed):
    scores = jnp.einsum(
        "qhd,khd->hqk", query_block, keys, preferred_element_type=jnp.float32
    ) * HEAD_DIM ** (-0.5)
    return jnp.where(allowed[None], scores, MASKED)


def attend_row(pieces):
    packed, seg_row = pieces
    query = packed[:, 0]
    keys = packed[:, 1]
    values = packed[:, 2]

    def one_block(start):
        allowed = allowed_pairs(seg_row, start, QBLOCK)
        query_block = lax.dynamic_slice_in_dim(query, start, QBLOCK, 0)
        scores = block_scores(query_block, keys, allowed)
        peak = jnp.max(scores, axis=-1, keepdims=True)
        expo = jnp.exp(scores - peak)
        total = jnp.sum(expo, axis=-1, keepdims=True)
        weights = (expo / total).astype(jnp.bfloat16)
        mixed = jnp.einsum("hqk,khd->qhd", weights, values, preferred_element_type=jnp.float32)
        return (mixed, (peak + jnp.log(total))[..., 0])

    starts = jnp.arange(packed.shape[0] // QBLOCK, dtype=jnp.int32) * QBLOCK
    mixed, logsum = lax.map(one_block, starts)
    return (mixed.reshape(keys.shape), logsum)


def attend_row_back(pieces):
    packed, logsum, grad_row, seg_row = pieces
    query = packed[:, 0]
    keys = packed[:, 1]
    values = packed[:, 2]
    factor = HEAD_DIM ** (-0.5)

    def one_block(carry, block_inputs):
        grad_keys, grad_values = carry
        start, lse_block = block_inputs
        allowed = allowed_pairs(seg_row, start, QBLOCK)
        query_block = lax.dynamic_slice_in_dim(query, start, QBLOCK, 0)
        grad_block = lax.dynamic_slice_in_dim(grad_row, start, QBLOCK, 0)
        scores = block_scores(query_block, keys, allowed)
        weights = jnp.exp(scores - lse_block[..., None])
        grad_weights = jnp.einsum(
            "qhd,khd->hqk", grad_block, values, preferred_element_type=jnp.float32
        )
        inner = jnp.sum(weights * grad_weights, axis=-1, keepdims=True)
        grad_scores = (weights * (grad_weights - inner)).astype(jnp.bfloat16)
        grad_query = (
            jnp.einsum("hqk,khd->qhd", grad_scores, keys, preferred_element_type=jnp.float32)
            * factor
        )
        grad_keys = (
            grad_keys
            + jnp.einsum(
                "hqk,qhd->khd", grad_scores, query_block, preferred_element_type=jnp.float32
            )
            * factor
        )
        grad_values = grad_values + jnp.einsum(
            "hqk,qhd->khd",
            weights.astype(jnp.bfloat16),
            grad_block,
            preferred_element_type=jnp.float32,
        )
        return ((grad_keys, grad_values), grad_query)

    starts = jnp.arange(packed.shape[0] // QBLOCK, dtype=jnp.int32) * QBLOCK
    zeros = jnp.zeros(keys.shape, jnp.float32)
    (grad_keys, grad_values), grad_query = lax.scan(one_block, (zeros, zeros), (starts, logsum))
    grad_query = grad_query.reshape(keys.shape)
    return jnp.stack([grad_query, grad_keys, grad_values], axis=1).astype(jnp.bfloat16)


def times_rows(activations, matrix):
    return lax.dot_general(
        activations,
        matrix,
        (((activations.ndim - 1,), (1,)), ((), ())),
        preferred_element_type=jnp.float32,
    )


def times_matrix(activations, matrix):
    return lax.dot_general(
        activations,
        matrix,
        (((activations.ndim - 1,), (0,)), ((), ())),
        preferred_element_type=jnp.float32,
    )


def weight_term(grads, activations):
    return jnp.einsum("rpe,rpd->ed", grads, activations, preferred_element_type=jnp.float32)


def body(
    inputs,
    segment_ids,
    w_qkv,
    w_out,
    w_up,
    w_down,
    gain_attn,
    gain_mix,
    gain_ffn,
    gain_hidden,
    cotangent,
):
    rows, local, width = inputs.shape
    groups = lax.axis_size("seq")
    length = local * groups
    heads_here = HEADS // groups
    group_width = heads_here * HEAD_DIM
    all_full = (
        lax.all_gather(w_qkv, "seq", axis=0, tiled=True),
        lax.all_gather(w_out, "seq", axis=0, tiled=True),
        lax.all_gather(w_up, "seq", axis=0, tiled=True),
        lax.all_gather(w_down, "seq", axis=0, tiled=True),
    )
    full_positions = jax.vmap(doc_positions)(segment_ids)
    positions = lax.dynamic_slice_in_dim(full_positions, lax.axis_index("seq") * local, local, 1)
    cosine, sine, growth = xpos_tables(positions)
    inputs_f32 = inputs.astype(jnp.float32)
    normed_f32, attn_pull = jax.vjp(norm_rows, inputs_f32, gain_attn)
    normed = normed_f32.astype(jnp.bfloat16)
    qkv = times_rows(normed, all_full[0]).reshape(rows, local, 3, HEADS, HEAD_DIM)
    query, query_pull = jax.vjp(lambda part: rotate(part, cosine, sine, growth), qkv[:, :, 0])
    keys, keys_pull = jax.vjp(lambda part: rotate(part, cosine, sine, 1.0 / growth), qkv[:, :, 1])
    stacked = jnp.stack([query, keys, qkv[:, :, 2]], axis=2).astype(jnp.bfloat16)
    stacked = stacked.reshape(rows, local, 3, groups, group_width)
    gathered = lax.all_to_all(stacked, "seq", split_axis=3, concat_axis=1, tiled=True)
    head_view = gathered.reshape(rows, length, 3, heads_here, HEAD_DIM)
    attended_heads, logsum = lax.map(attend_row, (head_view, segment_ids))
    attended_low = attended_heads.astype(jnp.bfloat16).reshape(rows, length, 1, group_width)
    returned = lax.all_to_all(attended_low, "seq", split_axis=1, concat_axis=2, tiled=True)
    attended = returned.reshape(rows, local, width).astype(jnp.float32)
    mix_f32, mix_pull = jax.vjp(norm_rows, attended, gain_mix)
    mix_in = mix_f32.astype(jnp.bfloat16)
    middle = inputs_f32 + times_rows(mix_in, all_full[1])
    ffn_f32, ffn_pull = jax.vjp(norm_rows, middle, gain_ffn)
    ffn_in = ffn_f32.astype(jnp.bfloat16)
    upper = times_rows(ffn_in, all_full[2])
    hidden_f32, hidden_pull = jax.vjp(gelu_norm, upper, gain_hidden)
    hidden = hidden_f32.astype(jnp.bfloat16)
    outputs = (middle + times_rows(hidden, all_full[3])).astype(jnp.bfloat16)
    back_full = (
        lax.all_gather(w_qkv, "seq", axis=0, tiled=True),
        lax.all_gather(w_out, "seq", axis=0, tiled=True),
        lax.all_gather(w_up, "seq", axis=0, tiled=True),
        lax.all_gather(w_down, "seq", axis=0, tiled=True),
    )
    grad_hidden_in = times_matrix(cotangent, back_full[3])
    grad_upper_f32, grad_gain_hidden = hidden_pull(grad_hidden_in)
    grad_upper = grad_upper_f32.astype(jnp.bfloat16)
    grad_ffn_in = times_matrix(grad_upper, back_full[2])
    grad_middle_part, grad_gain_ffn = ffn_pull(grad_ffn_in)
    grad_middle = cotangent.astype(jnp.float32) + grad_middle_part
    grad_branch = grad_middle.astype(jnp.bfloat16)
    grad_mix_in = times_matrix(grad_branch, back_full[1])
    grad_attended_f32, grad_gain_mix = mix_pull(grad_mix_in)
    grad_attended = grad_attended_f32.astype(jnp.bfloat16).reshape(rows, local, groups, group_width)
    grad_heads_view = lax.all_to_all(grad_attended, "seq", split_axis=2, concat_axis=1, tiled=True)
    grad_heads_view = grad_heads_view.reshape(rows, length, heads_here, HEAD_DIM)
    grad_packed = lax.map(attend_row_back, (head_view, logsum, grad_heads_view, segment_ids))
    grad_packed = grad_packed.reshape(rows, length, 3, 1, group_width)
    grad_local = lax.all_to_all(grad_packed, "seq", split_axis=1, concat_axis=3, tiled=True)
    grad_local = grad_local.reshape(rows, local, 3, HEADS, HEAD_DIM).astype(jnp.float32)
    grad_query_pre = query_pull(grad_local[:, :, 0])[0]
    grad_keys_pre = keys_pull(grad_local[:, :, 1])[0]
    grad_qkv = jnp.stack([grad_query_pre, grad_keys_pre, grad_local[:, :, 2]], axis=2)
    grad_qkv = grad_qkv.reshape(rows, local, 3 * width).astype(jnp.bfloat16)
    grad_normed = times_matrix(grad_qkv, back_full[0])
    grad_input_part, grad_gain_attn = attn_pull(grad_normed)
    grad_inputs = grad_middle + grad_input_part
    grad_w_down = lax.psum_scatter(
        weight_term(cotangent, hidden).astype(jnp.bfloat16), "seq", scatter_dimension=0, tiled=True
    ).astype(jnp.float32)
    grad_w_up = lax.psum_scatter(
        weight_term(grad_upper, ffn_in).astype(jnp.bfloat16), "seq", scatter_dimension=0, tiled=True
    ).astype(jnp.float32)
    grad_w_out = lax.psum_scatter(
        weight_term(grad_branch, mix_in).astype(jnp.bfloat16),
        "seq",
        scatter_dimension=0,
        tiled=True,
    ).astype(jnp.float32)
    grad_w_qkv = lax.psum_scatter(
        weight_term(grad_qkv, normed).astype(jnp.bfloat16), "seq", scatter_dimension=0, tiled=True
    ).astype(jnp.float32)
    grad_w_qkv, grad_w_out, grad_w_up, grad_w_down = (
        lax.psum(grad_w_qkv.astype(jnp.bfloat16), "batch").astype(jnp.float32),
        lax.psum(grad_w_out.astype(jnp.bfloat16), "batch").astype(jnp.float32),
        lax.psum(grad_w_up.astype(jnp.bfloat16), "batch").astype(jnp.float32),
        lax.psum(grad_w_down.astype(jnp.bfloat16), "batch").astype(jnp.float32),
    )
    grad_gain_attn, grad_gain_mix, grad_gain_ffn, grad_gain_hidden = lax.psum(
        (grad_gain_attn, grad_gain_mix, grad_gain_ffn, grad_gain_hidden), ("batch", "seq")
    )
    return (
        outputs,
        grad_inputs,
        grad_w_qkv,
        grad_w_out,
        grad_w_up,
        grad_w_down,
        grad_gain_attn,
        grad_gain_mix,
        grad_gain_ffn,
        grad_gain_hidden,
    )


def solution(mesh):
    in_specs = (
        P("batch", "seq", None),
        P("batch", None),
        P("seq", None),
        P("seq", None),
        P("seq", None),
        P("seq", None),
        P(),
        P(),
        P(),
        P(),
        P("batch", "seq", None),
    )
    out_specs = (
        P("batch", "seq", None),
        P("batch", "seq", None),
        P("seq", None),
        P("seq", None),
        P("seq", None),
        P("seq", None),
        P(),
        P(),
        P(),
        P(),
    )
    return jax.shard_map(body, mesh=mesh, in_specs=in_specs, out_specs=out_specs, check_vma=False)
```

profile of v0, /device:TPU:0, one launch (start us, length us, event | category | flops | bytes accessed | tf_op | source)
XLA Modules:
  0.0 2033.4 jit_solution(4240888310886022481)
XLA Ops:
  12.6 125.4 %all-gather.5.cloned.1.call-done = bf16[6144,2048]{1,0:T(8,128)(2,1)} async-done(((bf16[768,2048]{1,0:T(8,128)(2,1)}), bf16[6144,2048]{1,0:T(8,128)(2,1)}) %all-gather.5.cloned.1.call-update) | async-done | bytes 25165840 | tf_op jit(solution)/shard_map/all_gather | solution.py:181
  138.0 14.7 convolution_bitcast_fusion.2
  159.9 60.2 %all-to-all-done = bf16[1,256,3,8,256]{1,4,2,0,3:T(8,128)(2,1)S(1)} async-done(((bf16[1,256,3,8,256]{1,4,2,0,3:T(8,128)(2,1)}), bf16[1,256,3,8,256]{1,4,2,0,3:T(8,128)(2,1)S(1)}, u32[]{:S(2)}, u32[]{:S(2)}) %all-to-all-start) | async-done | bytes 3145760 | tf_op jit(solution)/shard_map/all_to_all | solution.py:197
  233.3 72.1 %while.45 = (s32[]{:T(128)}, bf16[4,512,4,64]{1,3,2,0:T(8,128)(2,1)}, f32[4,4,512]{2,1,0:T(4,128)}, s32[4]{0:T(128)S(1)}, s32[2048]{0:T(1024)S(1)}, /*index=5*/b...) while((s32[]{:T(128)}, ...), condition=%wide.region_7.8_spmd, body=%wide.region_4.7_spmd.sunk | while | flops 1127217664 | bytes 65882348 | solution.py:90
  318.4 12.8 reduce.36
  333.4 30.4 %all_to_all.49 = bf16[8,2,32768]{2,1,0:T(2,128)(2,1)S(1)} all-to-all(bf16[8,2,32768]{2,1,0:T(2,128)(2,1)} %reshape.1112), channel_id=1, replica_groups=mesh['batch'=4,'seq'=8] {'seq'}, dimensions={0} | all-to-all | bytes 2097152 | tf_op jit(solution)/shard_map/all_to_all | solution.py:201
  384.5 10.7 all-gather.9.cloned.1.call-done
  395.1 34.0 %fusion.87 = (f32[256]{0:T(256)S(1)}, f32[256,8192]{1,0:T(8,128)}, f32[256,8192]{1,0:T(8,128)}, f32[256,8192]{1,0:T(8,128)}) fusion(bf16[8192,2048]{1,0:T(8,128)(2,1)} %all-gather.9.cloned.1.call-done, f32[1,256,2048]{2,1,0:T(8,128)} %copy-done.9, f32[2048]{0:T(1024)S(1)} %copy-done.48, f32[256]{0:T(256)S(1)} %fusion.76, f32[256]{0:T(256)S(1)} %broadcast_multiply_fusion.1), kind=kOutput, calls=%fused_computation.193 | convolution fusion | flops 8728346624 | bytes 60828672 | tf_op jit(solution)/shard_map/dot_general | solution.py:141
  429.2 128.6 %all-gather.11.cloned.1.call-done = bf16[2048,8192]{1,0:T(8,128)(2,1)} async-done(((bf16[256,8192]{1,0:T(8,128)(2,1)}), bf16[2048,8192]{1,0:T(8,128)(2,1)}) %all-gather.11.cloned.1.call-update) | async-done | bytes 33554448 | tf_op jit(solution)/shard_map/all_gather | solution.py:184
  557.7 20.5 %multiply_reduce_fusion.2 = (f32[256]{0:T(256)S(1)}, f32[256]{0:T(256)S(1)}, f32[256,8192]{1,0:T(8,128)}) fusion(f32[256,8192]{1,0:T(8,128)} %get-tuple-element.328, f32[8192]{0:T(1024)S(1)} %copy-done.29, f32[256]{0:T(256)S(1)} %broadcast_multiply_fusion, bf16[2048,8192]{1,0:T(8,128)(2,1)} %all-gather.11.cloned.1.call-done, ...), kind=kOutput, calls=%fused_computation.55 | convolution fusion | flops 8602517504 | bytes 51416064 | tf_op jit(solution)/shard_map/dot_general | solution.py:150
  588.3 12.6 add_convert_fusion
  600.9 18.2 fusion.57
  656.8 246.3 %while.46 = (s32[]{:T(128)}, f32[2048,4,64]{0,2,1:T(8,128)}, f32[2048,4,64]{0,2,1:T(8,128)}, bf16[4,512,4,64]{1,3,2,0:T(8,128)(2,1)}, s32[4]{0:T(128)S(1)}, /*in...) while((s32[]{:T(128)}, f32[2048,4,64]{0,2,1:T(8,128)}, ...), condition=%wide.region_23.24_spmd.clone, body=%wide.region_21.23_spmd.clone.sunk | while | flops 2753165824 | bytes 193538464 | solution.py:135
  671.7 13.1 multiply_reduce_fusion.8
  684.8 15.7 multiply_convert_fusion.13
  733.9 12.5 multiply_reduce_fusion.8
  746.4 14.9 multiply_convert_fusion.13
  795.1 12.5 multiply_reduce_fusion.8
  807.6 14.9 multiply_convert_fusion.13
  856.2 12.5 multiply_reduce_fusion.8
  868.7 14.9 multiply_convert_fusion.13
  916.6 52.7 %all_to_all.48 = bf16[1,2048,3,1,256]{4,2,3,0,1:T(4,128)(2,1)S(1)} all-to-all(bf16[1,2048,3,1,256]{4,2,3,0,1:T(4,128)(2,1)} %copy.106), channel_id=1, replica_groups=mesh['batch'=4,'seq'=8] {'seq'}, dimensions={1} | all-to-all | bytes 6291456 | tf_op jit(solution)/shard_map/all_to_all | solution.py:232
  987.5 13.8 convolution_convert_fusion.1
  1002.5 26.2 %convert_bitcast_fusion = bf16[2048,8192]{0,1:T(8,128)(2,1)} fusion(bf16[1,256,2048]{2,1,0:T(8,128)(2,1)S(1)} %copy-done.14, f32[256,8192]{1,0:T(8,128)} %get-tuple-element.328, f32[8192]{0:T(1024)S(1)} %copy-done.30, f32[256]{0:T(256)S(1)} %copy-done.45, f32[256]{0:T(256)S(1)} %copy-done.43), kind=kOutput, calls=%fused_computation.47 | convolution fusion | flops 8615100416 | bytes 43026432 | tf_op jit(solution)/shard_map/rpe,rpd->ed/dot_general | solution.py:159
  1030.7 17.3 convolution_convert_fusion
  1048.1 109.3 %reduce-scatter.5.cloned.1.call-done = bf16[768,2048]{1,0:T(8,128)(2,1)} async-done(((bf16[6144,2048]{1,0:T(8,128)(2,1)}), bf16[768,2048]{1,0:T(8,128)(2,1)}) %reduce-scatter.5.cloned.1.call-update) | async-done | bytes 3145744 | tf_op jit(solution)/shard_map/reduce_scatter | solution.py:253
  1157.5 209.3 %reduce-scatter.11.cloned.1.call-done = bf16[256,8192]{0,1:T(8,128)(2,1)} async-done(((bf16[2048,8192]{0,1:T(8,128)(2,1)}), bf16[256,8192]{0,1:T(8,128)(2,1)}) %reduce-scatter.11.cloned.1.call-update) | async-done | bytes 4194320 | tf_op jit(solution)/shard_map/reduce_scatter | solution.py:241
  1366.8 208.8 %reduce-scatter.9.cloned.1.call-done = bf16[1024,2048]{1,0:T(8,128)(2,1)} async-done(((bf16[8192,2048]{1,0:T(8,128)(2,1)}), bf16[1024,2048]{1,0:T(8,128)(2,1)}) %reduce-scatter.9.cloned.1.call-update) | async-done | bytes 4194320 | tf_op jit(solution)/shard_map/reduce_scatter | solution.py:244
  1575.6 18.8 fusion.50
  1594.5 12.7 fusion.56
  1608.3 50.4 %all-reduce.4 = (f32[2048]{0:T(1024)}, f32[2048]{0:T(1024)}, f32[2048]{0:T(1024)}, f32[8192]{0:T(1024)}) all-reduce(f32[2048]{0:T(1024)S(1)} %get-tuple-element.275, f32[2048]{0:T(1024)S(1)} %copy-done.62, f32[2048]{0:T(1024)S(1)} %copy-done.61, f32[8192]{0:T(1024)S(1)} %copy-done.41), channel_id=1, replica_groups=mesh['batch'=4,'seq'=8] {'batch','seq'}, use_global_device_ids=true, to_apply=%region_35.36 | all-reduce | flops 14336 | bytes 114688 | tf_op jit(solution)/shard_map/psum | solution.py:262
  1662.8 345.2 %all-reduce.8.cloned.1.call-done = (bf16[256,8192]{0,1:T(8,128)(2,1)}, bf16[768,2048]{1,0:T(8,128)(2,1)}, bf16[256,2048]{1,0:T(8,128)(2,1)}, bf16[1024,2048]{1,0:T(8,128)(2,1)}) async-done(((bf16[256,8192]{0,1:T(8,128)(2,1)}, bf16[768,2048]{1,0:T(8,128)(2,1)}, bf16[256,2048]{1,0:T(8,128)(2,1)}, bf16[1024,2048]{1,0:T(8,128)(2,1)}), (bf16[256,8192]{0,1:T(8,128)(2,1)}, bf16[768,2048]{1,0:T(8,128)(2,1)}, ...) | async-done | bytes 12582928 | tf_op jit(solution)/shard_map/psum | solution.py:260
  (376 shorter events, 358.6 us)
Async XLA Ops:
  7.2 130.8 %all-gather.5.cloned.1.call-start = ((), (), s32[]{:S(2)}) async-start(), calls=%async_computation.8 | async-start | bytes 28311552 | tf_op jit(solution)/shard_map/all_gather | solution.py:181
  7.9 368.3 %all-gather.7.cloned.1.call-start = ((), (), s32[]{:S(2)}) async-start(), calls=%async_computation.9 | async-start | bytes 9437184 | tf_op jit(solution)/shard_map/all_gather | solution.py:182
  8.7 386.4 %all-gather.9.cloned.1.call-start = ((), (), s32[]{:S(2)}) async-start(), calls=%async_computation.10 | async-start | bytes 37748736 | tf_op jit(solution)/shard_map/all_gather | solution.py:183
  9.4 128.5 %copy-start.39 = (f32[2048]{0:T(1024)S(1)}, f32[2048]{0:T(1024)}, u32[]{:S(2)}) copy-start(f32[2048]{0:T(1024)} %param.21) | copy-start | bytes 24580
  9.4 548.3 %all-gather.11.cloned.1.call-start = ((), (), s32[]{:S(2)}) async-start(), calls=%async_computation.11 | async-start | bytes 37748736 | tf_op jit(solution)/shard_map/all_gather | solution.py:184
  11.2 141.4 %copy-start.46 = (f32[256]{0:T(256)}, f32[256]{0:T(256)S(1)}, u32[]{:S(2)}) copy-start(f32[256]{0:T(256)S(1)} %broadcast_multiply_fusion.3) | copy-start | bytes 3076
  11.7 140.9 %copy-start.51 = (f32[256]{0:T(256)}, f32[256]{0:T(256)S(1)}, u32[]{:S(2)}) copy-start(f32[256]{0:T(256)S(1)} %fusion.74) | copy-start | bytes 3076
  12.5 140.6 %copy-start.31 = (f32[256,32]{0,1:T(8,128)}, f32[256,32]{0,1:T(8,128)S(1)}, u32[]{:S(2)}) copy-start(f32[256,32]{0,1:T(8,128)S(1)} %get-tuple-element.355) | copy-start | bytes 98308
  12.5 140.6 %copy-start.33 = (f32[256,32]{0,1:T(8,128)}, f32[256,32]{0,1:T(8,128)S(1)}, u32[]{:S(2)}) copy-start(f32[256,32]{0,1:T(8,128)S(1)} %get-tuple-element.356) | copy-start | bytes 98308
  12.6 140.5 %copy-start.35 = (f32[256,32]{0,1:T(8,128)}, f32[256,32]{0,1:T(8,128)S(1)}, u32[]{:S(2)}) copy-start(f32[256,32]{0,1:T(8,128)S(1)} %get-tuple-element.353) | copy-start | bytes 98308
  12.6 140.5 %copy-start.37 = (f32[256,32]{0,1:T(8,128)}, f32[256,32]{0,1:T(8,128)S(1)}, u32[]{:S(2)}) copy-start(f32[256,32]{0,1:T(8,128)S(1)} %get-tuple-element.354) | copy-start | bytes 98308
  156.0 64.1 %all-to-all-start = ((bf16[1,256,3,8,256]{1,4,2,0,3:T(8,128)(2,1)}), bf16[1,256,3,8,256]{1,4,2,0,3:T(8,128)(2,1)S(1)}, u32[]{:S(2)}, u32[]{:S(2)}) async-start(bf16[1,256,3,8,256]{1,4,2,0,3:T(8,128)(2,1)} %pad_maximum_fusion), calls=%async_computation | async-start | bytes 6291456 | tf_op jit(solution)/shard_map/all_to_all | solution.py:197
  305.4 25.9 %copy-start = (bf16[2048,4,64]{0,2,1:T(8,128)(2,1)}, bf16[2048,4,64]{0,2,1:T(8,128)(2,1)S(1)}, u32[]{:S(2)}) copy-start(bf16[2048,4,64]{0,2,1:T(8,128)(2,1)S(1)} %get-tuple-element.584) | copy-start | bytes 3145732
  305.4 25.9 %copy-start.6 = (bf16[2048,4,64]{0,2,1:T(8,128)(2,1)}, bf16[2048,4,64]{0,2,1:T(8,128)(2,1)S(1)}, u32[]{:S(2)}) copy-start(bf16[2048,4,64]{0,2,1:T(8,128)(2,1)S(1)} %get-tuple-element.593) | copy-start | bytes 3145732
  305.4 25.9 %copy-start.8 = (bf16[2048,4,64]{0,2,1:T(8,128)(2,1)}, bf16[2048,4,64]{0,2,1:T(8,128)(2,1)S(1)}, u32[]{:S(2)}) copy-start(bf16[2048,4,64]{0,2,1:T(8,128)(2,1)S(1)} %get-tuple-element.595) | copy-start | bytes 3145732
  305.4 25.9 %copy-start.63 = (s32[4]{0:T(128)}, s32[4]{0:T(128)S(1)}, u32[]{:S(2)}) copy-start(s32[4]{0:T(128)S(1)} %get-tuple-element.627) | copy-start | bytes 52
  376.2 18.9 copy-start.48
  382.8 236.3 %copy-start.53 = (f32[256]{0:T(256)}, f32[256]{0:T(256)S(1)}, u32[]{:S(2)}) copy-start(f32[256]{0:T(256)S(1)} %broadcast_multiply_fusion.1) | copy-start | bytes 3076
  384.4 234.7 %copy-start.55 = (f32[256]{0:T(256)}, f32[256]{0:T(256)S(1)}, u32[]{:S(2)}) copy-start(f32[256]{0:T(256)S(1)} %fusion.76) | copy-start | bytes 3076
  384.4 173.3 %copy-start.13 = (bf16[1,256,2048]{2,1,0:T(8,128)(2,1)S(1)}, bf16[1,256,2048]{2,1,0:T(8,128)(2,1)}, u32[]{:S(2)}) copy-start(bf16[1,256,2048]{2,1,0:T(8,128)(2,1)} %param.25) | copy-start | bytes 3145732
  384.5 173.3 %copy-start.29 = (f32[8192]{0:T(1024)S(1)}, f32[8192]{0:T(1024)}, u32[]{:S(2)}) copy-start(f32[8192]{0:T(1024)} %param.24) | copy-start | bytes 98308
  429.2 159.1 %copy-start.42 = (f32[256]{0:T(256)}, f32[256]{0:T(256)S(1)}, u32[]{:S(2)}) copy-start(f32[256]{0:T(256)S(1)} %broadcast_multiply_fusion) | copy-start | bytes 3076
  632.7 19.8 all-to-all-start.2
  637.0 411.1 %reduce-scatter.7.cloned.1.call-start = ((), (), s32[]{:S(2)}) async-start(), calls=%async_computation.13 | async-start | bytes 9437184 | tf_op jit(solution)/shard_map/reduce_scatter | solution.py:247
  645.9 511.5 %reduce-scatter.5.cloned.1.call-start = ((), (), s32[]{:S(2)}) async-start(), calls=%async_computation.12 | async-start | bytes 28311552 | tf_op jit(solution)/shard_map/reduce_scatter | solution.py:253
  761.3 15.8 slice-start
  822.5 15.8 slice-start
  883.6 15.8 slice-start
  1001.3 365.5 %reduce-scatter.11.cloned.1.call-start = ((), (), s32[]{:S(2)}) async-start(), calls=%async_computation.15 | async-start | bytes 37748736 | tf_op jit(solution)/shard_map/reduce_scatter | solution.py:241
  1028.7 546.9 %reduce-scatter.9.cloned.1.call-start = ((), (), s32[]{:S(2)}) async-start(), calls=%async_computation.14 | async-start | bytes 37748736 | tf_op jit(solution)/shard_map/reduce_scatter | solution.py:244
  1048.1 959.9 %all-reduce.8.cloned.1.call-start = ((), (), s32[]{:S(2)}) async-start(), calls=%async_computation.16 | async-start | bytes 25165824 | tf_op jit(solution)/shard_map/psum | solution.py:260
  1594.5 64.2 %copy-start.58 = (f32[256]{0:T(256)S(1)}, f32[256]{0:T(256)}, u32[]{:S(2)}) copy-start(f32[256]{0:T(256)} %copy-done.57) | copy-start | bytes 3076
  (72 other events, 387.3 us)
Sparse Core Ops, SparseCore 0:
  9.9 128.0 all-gather.4
  139.8 76.6 all-gather.6
  218.4 176.6 all-gather.8
  396.9 160.8 all-gather.10
  646.0 72.5 reduce-scatter.6
  1001.4 156.0 reduce-scatter.4
  1161.5 205.2 reduce-scatter.10
  1370.3 205.2 reduce-scatter.8
  1578.8 429.1 all-reduce.7
where the time goes:
time: 2040 us; the launch traced here: 2030 us
  waiting for transfers between devices  1210 us (59%)
  matrix products  389 us (19%)
  other arithmetic  176 us (9%)
  blocking collectives  133 us (7%)
  local copies, waits for them, and re-layouts  88.6 us (4%)
    psum x1, waiting for transfers between devices, body(): lax.psum(grad_w_down.astype(jnp.bfloat16), 'batch').astype(jnp.float32)  345 us
    reduce_scatter x1, waiting for transfers between devices, body(): lax.psum_scatter(weight_term(cotangent, hidden).astype(jnp.bfloat16), 'se...  209 us
    reduce_scatter x1, waiting for transfers between devices, body(): lax.psum_scatter(weight_term(grad_upper, ffn_in).astype(jnp.bfloat16), 's...  209 us
    all_gather x1, waiting for transfers between devices, body(): lax.all_gather(w_down, 'seq', axis=0, tiled=True)  129 us
    all_gather x1, waiting for transfers between devices, body(): lax.all_gather(w_qkv, 'seq', axis=0, tiled=True)  125 us
    reduce_scatter x1, waiting for transfers between devices, body(): lax.psum_scatter(weight_term(grad_qkv, normed).astype(jnp.bfloat16), 'seq...  109 us
    dot_general x4, matrix products, times_rows(): lax.dot_general(activations, matrix, (((activations.ndim - 1,), (1,)), ((...  74 us
    dot_general x4, matrix products, weight_term(): jnp.einsum('rpe,rpd->ed', grads, activations, preferred_element_type=jnp....  63.1 us
  transfers between devices with their start and end apart: 11, of which 9 were waited for; matrix products, arithmetic and copies ran while one was open for 27% of the time, Pallas kernels for 0%

commit v1 on v0

--- a/solution.py
+++ b/solution.py
@@ -11,6 +11,19 @@
 XBASE = 512
 EPSILON = 1e-05
 MASKED = -1e30
+
+
+def gather_around(x, axis, dim):
+    ways = lax.axis_size(axis)
+    up = [(d, (d + 1) % ways) for d in range(ways)]
+    down = [(d, (d - 1) % ways) for d in range(ways)]
+    earlier, later = ([x], [x])
+    for _ in range(ways // 2):
+        earlier.append(lax.ppermute(earlier[-1], axis, up))
+    for _ in range((ways - 1) // 2):
+        later.append(lax.ppermute(later[-1], axis, down))
+    line = jnp.concatenate([*earlier[::-1], *later[1:]], axis=dim)
+    return jnp.roll(line, (lax.axis_index(axis) - ways // 2) * x.shape[dim], axis=dim)
 
 
 def norm_rows(values, gain):
@@ -178,7 +191,7 @@
     heads_here = HEADS // groups
     group_width = heads_here * HEAD_DIM
     all_full = (
-        lax.all_gather(w_qkv, "seq", axis=0, tiled=True),
+        gather_around(w_qkv, "seq", 0),
         lax.all_gather(w_out, "seq", axis=0, tiled=True),
         lax.all_gather(w_up, "seq", axis=0, tiled=True),
         lax.all_gather(w_down, "seq", axis=0, tiled=True),

time: 2040 us -> 2420 us (1.19)
  waiting for transfers between devices: 1210 us -> 1480 us
  local copies, waits for them, and re-layouts: 88.6 us -> 170 us
    ppermute x0 -> x7, waiting for transfers between devices: none -> 424 us  [the longest x4 424 us: gather_around(): earlier.append(lax.ppermute(earlier[-1], axis, up))]
    all_gather x1, waiting for transfers between devices: 129 us -> 0.02 us  [body(): lax.all_gather(w_down, 'seq', axis=0, tiled=True)]
    unnamed x128 -> x145, local copies, waits for them, and re-layouts: 21.6 us -> 76.9 us
  transfers between devices with their start and end apart: 11 -> 18, of which waited for: 9 -> 11; matrix products, arithmetic and copies ran while one was open for 27% -> 27% of each run, Pallas kernels for 0% -> 0%
where the time goes in v1:
time: 2420 us; the launch traced here: 2410 us
  waiting for transfers between devices  1480 us (61%)
  matrix products  411 us (17%)
  other arithmetic  174 us (7%)
  local copies, waits for them, and re-layouts  170 us (7%)
  blocking collectives  118 us (5%)
  starting transfers between devices  30.2 us (1%)
    ppermute x4, waiting for transfers between devices, gather_around(): earlier.append(lax.ppermute(earlier[-1], axis, up))  424 us
    psum x1, waiting for transfers between devices, body(): lax.psum(grad_w_down.astype(jnp.bfloat16), 'batch').astype(jnp.float32)  369 us
    reduce_scatter x1, waiting for transfers between devices, body(): lax.psum_scatter(weight_term(grad_upper, ffn_in).astype(jnp.bfloat16), 's...  209 us
    reduce_scatter x1, waiting for transfers between devices, body(): lax.psum_scatter(weight_term(cotangent, hidden).astype(jnp.bfloat16), 'se...  209 us
    reduce_scatter x1, waiting for transfers between devices, body(): lax.psum_scatter(weight_term(grad_qkv, normed).astype(jnp.bfloat16), 'seq...  110 us
    all_gather x1, waiting for transfers between devices, body(): lax.all_gather(w_qkv, 'seq', axis=0, tiled=True)  107 us
    unnamed x145, local copies, waits for them, and re-layouts  76.9 us
    dot_general x4, matrix products, times_rows(): lax.dot_general(activations, matrix, (((activations.ndim - 1,), (1,)), ((...  75.9 us
  transfers between devices with their start and end apart: 18, of which 11 were waited for; matrix products, arithmetic and copies ran while one was open for 27% of the time, Pallas kernels for 0%

profile of v1, /device:TPU:0, one launch (start us, length us, event | category | flops | bytes accessed | tf_op | source)
XLA Modules:
  0.0 2413.0 jit_solution(7680290690394493305)
XLA Ops:
  9.9 70.3 %collective-permute-done = bf16[768,2048]{1,0:T(8,128)(2,1)S(1)} collective-permute-done((bf16[768,2048]{1,0:T(8,128)(2,1)}, bf16[768,2048]{1,0:T(8,128)(2,1)S(1)}, u32[]{:S(2)}, u32[]{:S(2)}) %collective-permute-start) | collective-permute-done | bytes 3145760 | tf_op jit(solution)/shard_map/ppermute | solution.py:22
  84.5 110.1 %collective-permute-done.1 = bf16[768,2048]{1,0:T(8,128)(2,1)S(1)} collective-permute-done((bf16[768,2048]{1,0:T(8,128)(2,1)S(1)}, bf16[768,2048]{1,0:T(8,128)(2,1)S(1)}, u32[]{:S(2)}, u32[]{:S(2)}) %collective-permute-start.1) | collective-permute-done | bytes 3145760 | tf_op jit(solution)/shard_map/ppermute | solution.py:22
  203.2 131.2 %collective-permute-done.2 = bf16[768,2048]{1,0:T(8,128)(2,1)} collective-permute-done((bf16[768,2048]{1,0:T(8,128)(2,1)S(1)}, bf16[768,2048]{1,0:T(8,128)(2,1)}, u32[]{:S(2)}, u32[]{:S(2)}) %collective-permute-start.2) | collective-permute-done | bytes 3145760 | tf_op jit(solution)/shard_map/ppermute | solution.py:22
  342.3 111.9 %collective-permute-done.3 = bf16[768,2048]{1,0:T(8,128)(2,1)} collective-permute-done((bf16[768,2048]{1,0:T(8,128)(2,1)}, bf16[768,2048]{1,0:T(8,128)(2,1)}, u32[]{:S(2)}, u32[]{:S(2)}) %collective-permute-start.3) | collective-permute-done | bytes 3145760 | tf_op jit(solution)/shard_map/ppermute | solution.py:22
  508.8 22.5 constant_dynamic-slice_fusion
  531.4 14.9 convolution_bitcast_fusion.2
  559.8 41.9 %all-to-all-done = bf16[1,256,3,8,256]{1,4,2,0,3:T(8,128)(2,1)S(1)} async-done(((bf16[1,256,3,8,256]{1,4,2,0,3:T(8,128)(2,1)}), bf16[1,256,3,8,256]{1,4,2,0,3:T(8,128)(2,1)S(1)}, u32[]{:S(2)}, u32[]{:S(2)}) %all-to-all-start) | async-done | bytes 3145760 | tf_op jit(solution)/shard_map/all_to_all | solution.py:210
  614.1 75.0 %while.45 = (s32[]{:T(128)}, bf16[4,512,4,64]{1,3,2,0:T(8,128)(2,1)}, f32[4,4,512]{2,1,0:T(4,128)}, s32[4]{0:T(128)S(1)}, s32[2048]{0:T(1024)S(1)}, /*index=5*/b...) while((s32[]{:T(128)}, ...), condition=%wide.region_7.8_spmd, body=%wide.region_4.7_spmd.sunk | while | flops 1127217664 | bytes 57494696 | solution.py:103
  702.1 12.6 reduce.36
  716.9 19.8 all_to_all.49
  759.9 34.1 %fusion.87 = (f32[256]{0:T(256)S(1)}, f32[256,8192]{1,0:T(8,128)}, f32[256,8192]{1,0:T(8,128)}, f32[256,8192]{1,0:T(8,128)}) fusion(bf16[8192,2048]{1,0:T(8,128)(2,1)} %all-gather.7.cloned.1.call-done, f32[1,256,2048]{2,1,0:T(8,128)} %copy-done.11, f32[2048]{0:T(1024)S(1)} %copy-done.48, f32[256]{0:T(256)S(1)} %fusion.76, f32[256]{0:T(256)S(1)} %broadcast_multiply_fusion.1), kind=kOutput, calls=%fused_computation.210 | convolution fusion | flops 8728346624 | bytes 60828672 | tf_op jit(solution)/shard_map/dot_general | solution.py:154
  794.1 20.5 multiply_reduce_fusion.2
  824.6 12.7 add_convert_fusion
  837.4 18.1 fusion.57
  892.9 261.8 %while.46 = (s32[]{:T(128)}, f32[2048,4,64]{0,2,1:T(8,128)}, f32[2048,4,64]{0,2,1:T(8,128)}, bf16[4,512,4,64]{1,3,2,0:T(8,128)(2,1)}, s32[4]{0:T(128)S(1)}, /*in...) while((s32[]{:T(128)}, f32[2048,4,64]{0,2,1:T(8,128)}, ...), condition=%wide.region_23.24_spmd.clone, body=%wide.region_21.23_spmd.clone.sunk | while | flops 2753165824 | bytes 185149760 | solution.py:148
  907.7 13.1 multiply_reduce_fusion.8
  920.8 15.7 multiply_convert_fusion.13
  986.5 14.9 multiply_convert_fusion.13
  1051.5 14.9 multiply_convert_fusion.13
  1116.5 14.9 multiply_convert_fusion.13
  1168.2 52.7 %all_to_all.48 = bf16[1,2048,3,1,256]{4,2,3,0,1:T(4,128)(2,1)S(1)} all-to-all(bf16[1,2048,3,1,256]{4,2,3,0,1:T(4,128)(2,1)} %copy.106), channel_id=1, replica_groups=mesh['batch'=4,'seq'=8] {'seq'}, dimensions={1} | all-to-all | bytes 6291456 | tf_op jit(solution)/shard_map/all_to_all | solution.py:245
  1239.0 13.9 convolution_convert_fusion.1
  1254.5 24.2 %convolution_convert_fusion = bf16[8192,2048]{1,0:T(8,128)(2,1)} fusion(bf16[256,8192]{1,0:T(8,128)(2,1)} %add_convert_fusion, f32[1,256,2048]{2,1,0:T(8,128)S(1)} %copy-done.13, f32[2048]{0:T(1024)S(1)} %copy-done.49, f32[256]{0:T(256)S(1)} %copy-done.56, f32[256]{0:T(256)S(1)} %copy-done.54), kind=kOutput, calls=%fused_computation.48 | convolution fusion | flops 8608808960 | bytes 39856128 | tf_op jit(solution)/shard_map/rpe,rpd->ed/dot_general | solution.py:172
  1279.5 19.4 convert_bitcast_fusion
  1299.7 109.6 %reduce-scatter.5.cloned.1.call-done = bf16[768,2048]{1,0:T(8,128)(2,1)} async-done(((bf16[6144,2048]{1,0:T(8,128)(2,1)}), bf16[768,2048]{1,0:T(8,128)(2,1)}) %reduce-scatter.5.cloned.1.call-update) | async-done | bytes 3145744 | tf_op jit(solution)/shard_map/reduce_scatter | solution.py:266
  1409.3 209.1 %reduce-scatter.9.cloned.1.call-done = bf16[1024,2048]{1,0:T(8,128)(2,1)} async-done(((bf16[8192,2048]{1,0:T(8,128)(2,1)}), bf16[1024,2048]{1,0:T(8,128)(2,1)}) %reduce-scatter.9.cloned.1.call-update) | async-done | bytes 4194320 | tf_op jit(solution)/shard_map/reduce_scatter | solution.py:257
  1618.5 208.9 %reduce-scatter.11.cloned.1.call-done = bf16[256,8192]{0,1:T(8,128)(2,1)} async-done(((bf16[2048,8192]{0,1:T(8,128)(2,1)}), bf16[256,8192]{0,1:T(8,128)(2,1)}) %reduce-scatter.11.cloned.1.call-update) | async-done | bytes 4194320 | tf_op jit(solution)/shard_map/reduce_scatter | solution.py:254
  1827.4 20.4 fusion.50
  1847.8 106.9 %all-gather.11.cloned.1.call-done = bf16[6144,2048]{1,0:T(8,128)(2,1)} async-done(((bf16[768,2048]{1,0:T(8,128)(2,1)}), bf16[6144,2048]{1,0:T(8,128)(2,1)}) %all-gather.11.cloned.1.call-update) | async-done | bytes 25165840 | tf_op jit(solution)/shard_map/all_gather | solution.py:226
  1954.7 13.1 fusion.56
  1968.9 45.4 %all-reduce.4 = (f32[2048]{0:T(1024)}, f32[2048]{0:T(1024)}, f32[2048]{0:T(1024)}, f32[8192]{0:T(1024)}) all-reduce(f32[2048]{0:T(1024)S(1)} %get-tuple-element.275, f32[2048]{0:T(1024)S(1)} %copy-done.62, f32[2048]{0:T(1024)S(1)} %copy-done.61, f32[8192]{0:T(1024)S(1)} %copy-done.41), channel_id=1, replica_groups=mesh['batch'=4,'seq'=8] {'batch','seq'}, use_global_device_ids=true, to_apply=%region_35.36 | all-reduce | flops 14336 | bytes 114688 | tf_op jit(solution)/shard_map/psum | solution.py:275
  2018.4 368.7 %all-reduce.8.cloned.1.call-done = (bf16[256,8192]{0,1:T(8,128)(2,1)}, bf16[768,2048]{1,0:T(8,128)(2,1)}, bf16[256,2048]{1,0:T(8,128)(2,1)}, bf16[1024,2048]{1,0:T(8,128)(2,1)}) async-done(((bf16[256,8192]{0,1:T(8,128)(2,1)}, bf16[768,2048]{1,0:T(8,128)(2,1)}, bf16[256,2048]{1,0:T(8,128)(2,1)}, bf16[1024,2048]{1,0:T(8,128)(2,1)}), (bf16[256,8192]{0,1:T(8,128)(2,1)}, bf16[768,2048]{1,0:T(8,128)(2,1)}, ...) | async-done | bytes 12582928 | tf_op jit(solution)/shard_map/psum | solution.py:273
  (364 shorter events, 495.2 us)
Async XLA Ops:
  7.2 330.7 %copy-start.26 = (s32[1,2048]{1,0:T(1,128)S(1)}, s32[1,2048]{1,0:T(1,128)}, u32[]{:S(2)}) copy-start(s32[1,2048]{1,0:T(1,128)} %param.16) | copy-start | bytes 24580
  7.2 331.6 %copy-start.4 = (bf16[1,256,2048]{2,1,0:T(8,128)(2,1)S(1)}, bf16[1,256,2048]{2,1,0:T(8,128)(2,1)}, u32[]{:S(2)}) copy-start(bf16[1,256,2048]{2,1,0:T(8,128)(2,1)} %param.15) | copy-start | bytes 3145732
  7.2 744.4 %all-gather.5.cloned.1.call-start = ((), (), s32[]{:S(2)}) async-start(), calls=%async_computation.8 | async-start | bytes 9437184 | tf_op jit(solution)/shard_map/all_gather | solution.py:195
  7.9 752.0 %all-gather.7.cloned.1.call-start = ((), (), s32[]{:S(2)}) async-start(), calls=%async_computation.9 | async-start | bytes 37748736 | tf_op jit(solution)/shard_map/all_gather | solution.py:196
  8.7 785.4 %all-gather.9.cloned.1.call-start = ((), (), s32[]{:S(2)}) async-start(), calls=%async_computation.10 | async-start | bytes 37748736 | tf_op jit(solution)/shard_map/all_gather | solution.py:197
  9.4 70.8 %collective-permute-start = (bf16[768,2048]{1,0:T(8,128)(2,1)}, bf16[768,2048]{1,0:T(8,128)(2,1)S(1)}, u32[]{:S(2)}, u32[]{:S(2)}) collective-permute-start(bf16[768,2048]{1,0:T(8,128)(2,1)} %param.17), channel_id=1, source_target_pairs={{0,1},{1,2},{2,3},{3,4},{4,5},{5,6},{6,7},{7,0},{8,9},{9,10},{10,1... | collective-permute-start | bytes 9437192 | tf_op jit(solution)/shard_map/ppermute | solution.py:22
  81.8 112.8 %collective-permute-start.1 = (bf16[768,2048]{1,0:T(8,128)(2,1)S(1)}, bf16[768,2048]{1,0:T(8,128)(2,1)S(1)}, u32[]{:S(2)}, u32[]{:S(2)}) collective-permute-start(bf16[768,2048]{1,0:T(8,128)(2,1)S(1)} %collective-permute-done), channel_id=1, source_target_pairs={{0,1},{1,2},{2,3},{3,4},{4,5},{5,6},{6,7},{7,0},{8,9},{9,10},{10,1... | collective-permute-start | bytes 9437192 | tf_op jit(solution)/shard_map/ppermute | solution.py:22
  82.4 118.5 %collective-permute-start.4 = (bf16[768,2048]{1,0:T(8,128)(2,1)}, bf16[768,2048]{1,0:T(8,128)(2,1)}, u32[]{:S(2)}, u32[]{:S(2)}) collective-permute-start(bf16[768,2048]{1,0:T(8,128)(2,1)} %param.17), channel_id=1, source_target_pairs={{0,7},{1,0},{2,1},{3,2},{4,3},{5,4},{6,5},{7,6},{8,15},{9,8},{10,9... | collective-permute-start | bytes 9437192 | tf_op jit(solution)/shard_map/ppermute | solution.py:24
  196.7 137.8 %collective-permute-start.2 = (bf16[768,2048]{1,0:T(8,128)(2,1)S(1)}, bf16[768,2048]{1,0:T(8,128)(2,1)}, u32[]{:S(2)}, u32[]{:S(2)}) collective-permute-start(bf16[768,2048]{1,0:T(8,128)(2,1)S(1)} %collective-permute-done.1), channel_id=1, source_target_pairs={{0,1},{1,2},{2,3},{3,4},{4,5},{5,6},{6,7},{7,0},{8,9},{9,10},{10,1... | collective-permute-start | bytes 9437192 | tf_op jit(solution)/shard_map/ppermute | solution.py:22
  200.9 138.5 %collective-permute-start.5 = (bf16[768,2048]{1,0:T(8,128)(2,1)}, bf16[768,2048]{1,0:T(8,128)(2,1)}, u32[]{:S(2)}, u32[]{:S(2)}) collective-permute-start(bf16[768,2048]{1,0:T(8,128)(2,1)} %collective-permute-done.4), channel_id=1, source_target_pairs={{0,7},{1,0},{2,1},{3,2},{4,3},{5,4},{6,5},{7,6},{8,15},{9,8},{10,9... | collective-permute-start | bytes 9437192 | tf_op jit(solution)/shard_map/ppermute | solution.py:24
  334.5 119.8 %collective-permute-start.3 = (bf16[768,2048]{1,0:T(8,128)(2,1)}, bf16[768,2048]{1,0:T(8,128)(2,1)}, u32[]{:S(2)}, u32[]{:S(2)}) collective-permute-start(bf16[768,2048]{1,0:T(8,128)(2,1)} %collective-permute-done.2), channel_id=1, source_target_pairs={{0,1},{1,2},{2,3},{3,4},{4,5},{5,6},{6,7},{7,0},{8,9},{9,10},{10,1... | collective-permute-start | bytes 9437192 | tf_op jit(solution)/shard_map/ppermute | solution.py:22
  339.0 192.4 %copy-start.46 = (f32[256]{0:T(256)}, f32[256]{0:T(256)S(1)}, u32[]{:S(2)}) copy-start(f32[256]{0:T(256)S(1)} %broadcast_multiply_fusion.3) | copy-start | bytes 3076
  339.5 137.5 %collective-permute-start.6 = (bf16[768,2048]{1,0:T(8,128)(2,1)}, bf16[768,2048]{1,0:T(8,128)(2,1)}, u32[]{:S(2)}, u32[]{:S(2)}) collective-permute-start(bf16[768,2048]{1,0:T(8,128)(2,1)} %collective-permute-done.5), channel_id=1, source_target_pairs={{0,7},{1,0},{2,1},{3,2},{4,3},{5,4},{6,5},{7,6},{8,15},{9,8},{10,9... | collective-permute-start | bytes 9437192 | tf_op jit(solution)/shard_map/ppermute | solution.py:24
  341.8 120.4 %copy-start.18 = (bf16[768,2048]{1,0:T(8,128)(2,1)S(1)}, bf16[768,2048]{1,0:T(8,128)(2,1)}, u32[]{:S(2)}) copy-start(bf16[768,2048]{1,0:T(8,128)(2,1)} %copy-done.17) | copy-start | bytes 9437188
  341.9 189.5 %copy-start.51 = (f32[256]{0:T(256)}, f32[256]{0:T(256)S(1)}, u32[]{:S(2)}) copy-start(f32[256]{0:T(256)S(1)} %fusion.74) | copy-start | bytes 3076
  342.2 204.5 %copy-start.31 = (f32[256,32]{0,1:T(8,128)}, f32[256,32]{0,1:T(8,128)S(1)}, u32[]{:S(2)}) copy-start(f32[256,32]{0,1:T(8,128)S(1)} %get-tuple-element.355) | copy-start | bytes 98308
  342.2 204.5 %copy-start.33 = (f32[256,32]{0,1:T(8,128)}, f32[256,32]{0,1:T(8,128)S(1)}, u32[]{:S(2)}) copy-start(f32[256,32]{0,1:T(8,128)S(1)} %get-tuple-element.356) | copy-start | bytes 98308
  342.3 204.4 %copy-start.35 = (f32[256,32]{0,1:T(8,128)}, f32[256,32]{0,1:T(8,128)S(1)}, u32[]{:S(2)}) copy-start(f32[256,32]{0,1:T(8,128)S(1)} %get-tuple-element.353) | copy-start | bytes 98308
  342.3 204.4 %copy-start.37 = (f32[256,32]{0,1:T(8,128)}, f32[256,32]{0,1:T(8,128)S(1)}, u32[]{:S(2)}) copy-start(f32[256,32]{0,1:T(8,128)S(1)} %get-tuple-element.354) | copy-start | bytes 98308
  342.3 122.1 %copy-start.16 = (bf16[768,2048]{1,0:T(8,128)(2,1)S(1)}, bf16[768,2048]{1,0:T(8,128)(2,1)}, u32[]{:S(2)}) copy-start(bf16[768,2048]{1,0:T(8,128)(2,1)} %copy-done.15) | copy-start | bytes 9437188
  549.6 52.1 %all-to-all-start = ((bf16[1,256,3,8,256]{1,4,2,0,3:T(8,128)(2,1)}), bf16[1,256,3,8,256]{1,4,2,0,3:T(8,128)(2,1)S(1)}, u32[]{:S(2)}, u32[]{:S(2)}) async-start(bf16[1,256,3,8,256]{1,4,2,0,3:T(8,128)(2,1)} %pad_maximum_fusion), calls=%async_computation | async-start | bytes 6291456 | tf_op jit(solution)/shard_map/all_to_all | solution.py:210
  868.9 19.7 all-to-all-start.2
  873.2 426.5 %reduce-scatter.7.cloned.1.call-start = ((), (), s32[]{:S(2)}) async-start(), calls=%async_computation.13 | async-start | bytes 9437184 | tf_op jit(solution)/shard_map/reduce_scatter | solution.py:260
  882.0 527.4 %reduce-scatter.5.cloned.1.call-start = ((), (), s32[]{:S(2)}) async-start(), calls=%async_computation.12 | async-start | bytes 28311552 | tf_op jit(solution)/shard_map/reduce_scatter | solution.py:266
  1252.9 365.6 %reduce-scatter.9.cloned.1.call-start = ((), (), s32[]{:S(2)}) async-start(), calls=%async_computation.14 | async-start | bytes 37748736 | tf_op jit(solution)/shard_map/reduce_scatter | solution.py:257
  1278.7 548.6 %reduce-scatter.11.cloned.1.call-start = ((), (), s32[]{:S(2)}) async-start(), calls=%async_computation.15 | async-start | bytes 37748736 | tf_op jit(solution)/shard_map/reduce_scatter | solution.py:254
  1298.9 655.8 %all-gather.11.cloned.1.call-start = ((), (), s32[]{:S(2)}) async-start(), calls=%async_computation.11 | async-start | bytes 28311552 | tf_op jit(solution)/shard_map/all_gather | solution.py:226
  1299.7 1087.5 %all-reduce.8.cloned.1.call-start = ((), (), s32[]{:S(2)}) async-start(), calls=%async_computation.16 | async-start | bytes 25165824 | tf_op jit(solution)/shard_map/psum | solution.py:273
  1847.8 121.1 %copy-start.41 = (f32[8192]{0:T(1024)S(1)}, f32[8192]{0:T(1024)}, u32[]{:S(2)}) copy-start(f32[8192]{0:T(1024)} %get-tuple-element.267) | copy-start | bytes 98308
  1847.8 121.1 %copy-start.61 = (f32[2048]{0:T(1024)S(1)}, f32[2048]{0:T(1024)}, u32[]{:S(2)}) copy-start(f32[2048]{0:T(1024)} %get-tuple-element.271) | copy-start | bytes 24580
  1847.8 121.1 %copy-start.62 = (f32[2048]{0:T(1024)S(1)}, f32[2048]{0:T(1024)}, u32[]{:S(2)}) copy-start(f32[2048]{0:T(1024)} %get-tuple-element.273) | copy-start | bytes 24580
  1847.8 166.5 %copy-start.58 = (f32[256]{0:T(256)S(1)}, f32[256]{0:T(256)}, u32[]{:S(2)}) copy-start(f32[256]{0:T(256)} %copy-done.57) | copy-start | bytes 3076
  (60 other events, 904.5 us)
Sparse Core Ops, SparseCore 0:
  9.9 73.9 all-gather.4
  85.8 285.4 all-gather.6
  373.2 201.4 all-gather.8
  882.1 72.5 reduce-scatter.6
  1253.0 156.2 reduce-scatter.4
  1413.2 205.2 reduce-scatter.8
  1622.0 205.2 reduce-scatter.10
  1829.4 125.2 all-gather.10
  1957.9 429.1 all-reduce.7
